TPU v7x, 32 devices: a whole 2x2x4 slice. The times are simulated.
32 devices in a mesh: shot: 2 (over x), gz: 16 (over z, y, core).
Axes of the slice: x: 2, y: 2, z: 4, core: 2. Of those that a mesh axis runs over, the one named last changes fastest.
Arguments:
- source_now: float32 [256, 128, 128], P(('shot', 'gz')), parts along dimension 0, may hold values from -6 to 6
- source_before: float32 [256, 128, 128], P(('shot', 'gz')), parts along dimension 0, may hold values from -6 to 6
- receiver_now: float32 [256, 128, 128], P(('shot', 'gz')), parts along dimension 0, may hold values from -6 to 6
- receiver_before: float32 [256, 128, 128], P(('shot', 'gz')), parts along dimension 0, may hold values from -6 to 6
- speed_term: float32 [128, 128, 128], P('gz'), may hold values from 0.03 to 0.18
- saved_faces: float32 [24, 8, 128, 128], P('shot', None, 'gz'), parts along dimension 0, may hold values from -6 to 6
- face_steps: int32 [12], replicated, may hold values from 0 to 11, each once
- traces: bfloat16 [24, 128, 128], P('shot'), parts along dimension 0, may hold values from -6 to 6
- lag_offsets: int32 [8], replicated, may hold values from -8 to 8, as said below
- snap_phase: int32 [2], replicated, may hold values from 0 to 5
Outputs:
- image_out: bfloat16 [16, 128, 128, 128], P('shot', None, 'gz'), parts along dimension 0
- source_final: float32 [256, 128, 128], P(('shot', 'gz')), parts along dimension 0
- receiver_final: float32 [256, 128, 128], P(('shot', 'gz')), parts along dimension 0
There are 2 independent parts, one for each index of `shot`. A program takes and returns all parts, laid end to end along the dimension named above; an argument that names none is the same for every part. Nothing has to cross between parts.
Inputs may be any that keep to these rules, and one draw needn't show every extreme that they name: `face_steps`: each of the 12 saved slots belongs to exactly one step. `lag_offsets`: the 8 offsets are different, and both ends of the range occur.
All inputs are finite; a program needn't handle non-finite values.
Results may differ from a plain program's by a relative error of at most 0.001.
Values sent between devices are 32-bit elements; how exact they have to be, the bound alone decides.
No kernel may reach another device: no remote copies, remote signals or barrier semaphores. Data moves between devices by JAX's collectives and lax.ppermute only.
A program may use at most 64 MiB of HBM per device.

v0:
```python
import math
import jax
import jax.numpy as jnp
from jax import lax
from jax.sharding import PartitionSpec as P

LAGS = 8
LMAX = 8
SNAP_EVERY = 6
SNAPS = 2
stencil_weights = (-205.0 / 72.0, 8.0 / 5.0, -1.0 / 5.0, 8.0 / 315.0, -1.0 / 560.0)
damping = 0.25
smoothing = 16.0


def extended_2(block, sides, width):
    for axis, dim in sides:
        count = lax.axis_size(axis)
        forward = [(i, i + 1) for i in range(count - 1)]
        backward = [(target, source) for source, target in forward]
        low = lax.ppermute(
            lax.slice_in_dim(block, block.shape[dim] - width, None, axis=dim), axis, forward
        )
        high = lax.ppermute(lax.slice_in_dim(block, 0, width, axis=dim), axis, backward)
        block = jnp.concatenate([low, block, high], axis=dim)
    return block


def stencil(extended, layers):
    center = extended[:, 4 : 4 + layers]
    height = center.shape[2]
    breadth = center.shape[3]
    padded = jnp.pad(center, ((0, 0), (0, 0), (4, 4), (4, 4)))
    summed = 3.0 * stencil_weights[0] * center
    for offset in range(1, 5):
        weight = stencil_weights[offset]
        summed = summed + weight * (
            extended[:, 4 + offset : 4 + offset + layers]
            + extended[:, 4 - offset : 4 - offset + layers]
        )
        summed = summed + weight * (
            padded[:, :, 4 + offset : 4 + offset + height, 4 : 4 + breadth]
            + padded[:, :, 4 - offset : 4 - offset + height, 4 : 4 + breadth]
        )
        summed = summed + weight * (
            padded[:, :, 4 : 4 + height, 4 + offset : 4 + offset + breadth]
            + padded[:, :, 4 : 4 + height, 4 - offset : 4 - offset + breadth]
        )
    return summed


def advance(extended, center, previous, speed_term, faces_now, trace_now, top_row, layers):
    updated = 2.0 * center - previous + speed_term * stencil(extended, layers)
    breadth = updated.shape[3]
    column = lax.broadcasted_iota(jnp.int32, (8, breadth), 1)
    which = lax.broadcasted_iota(jnp.int32, (8, breadth), 0)
    target = jnp.where(which < 4, which, which + breadth - 8)
    placing = (column == target).astype(jnp.float32)
    boundary = jnp.einsum("fzy,fx->zyx", faces_now, placing, precision=lax.Precision.HIGHEST)
    x_index = lax.broadcasted_iota(jnp.int32, (1, 1, breadth), 2)
    edge_mask = (x_index < 4) | (x_index >= breadth - 4)
    source = jnp.where(edge_mask, boundary, updated[0])
    top_mask = lax.broadcasted_iota(jnp.int32, (layers, 1, 1), 0) == top_row
    receiver = updated[1] + jnp.where(top_mask, trace_now[None], 0.0)
    return jnp.stack([source, receiver])


def lag_images(snapshot, lag_offsets):
    source = snapshot[0]
    receiver = snapshot[1]
    margin = ((0, 0), (0, 0), (LMAX, LMAX))
    source_pad = jnp.pad(source, margin)
    receiver_pad = jnp.pad(receiver, margin)
    breadth = source.shape[2]
    images = []
    for lag_index in range(LAGS):
        lag_now = lag_offsets[lag_index]
        shifted_source = lax.dynamic_slice_in_dim(source_pad, LMAX - lag_now, breadth, 2)
        shifted_receiver = lax.dynamic_slice_in_dim(receiver_pad, LMAX + lag_now, breadth, 2)
        images.append(shifted_source * shifted_receiver)
    return (jnp.stack(images), source * source)


def depth_inverse(layers):
    ratio = (1.0 + 2.0 * smoothing) / (2.0 * smoothing)
    theta = math.log(ratio + math.sqrt(ratio * ratio - 1.0))
    hyper_sine = 0.5 * (math.exp(theta) - math.exp(-theta))
    scale = 1.0 / (2.0 * smoothing * hyper_sine * (1.0 - math.exp(-2.0 * (layers + 1) * theta)))
    row_index = lax.broadcasted_iota(jnp.int32, (layers, layers), 0)
    col_index = lax.broadcasted_iota(jnp.int32, (layers, layers), 1)
    apart = jnp.abs(row_index - col_index).astype(jnp.float32)
    joined = (row_index + col_index).astype(jnp.float32)
    total = float(layers)
    green = (
        jnp.exp(-theta * apart)
        - jnp.exp(-theta * (2.0 * total - joined))
        - jnp.exp(-theta * (joined + 2.0))
        + jnp.exp(-theta * (2.0 * total + 2.0 - apart))
    )
    return green * scale


def finish(raw_image, illumination):
    layers = illumination.shape[0]
    columns = illumination.reshape(layers, -1)
    inverse = depth_inverse(layers)
    smooth = jnp.dot(
        inverse, columns, precision=lax.Precision.HIGHEST, preferred_element_type=jnp.float32
    ).reshape(illumination.shape)
    return (raw_image / (smooth + damping)).astype(jnp.bfloat16)


def local(
    source_now,
    source_before,
    receiver_now,
    receiver_before,
    speed_term,
    saved_faces,
    face_steps,
    traces,
    lag_offsets,
    snap_phase,
):
    current = jnp.stack([source_now, receiver_now])
    previous = jnp.stack([source_before, receiver_before])
    layers = source_now.shape[0]
    is_top = lax.axis_index("gz") == 0
    top_row = jnp.where(is_top, 0, -1)
    raw_image = jnp.zeros((1,), jnp.float32)
    illumination = jnp.zeros((1,), jnp.float32)
    for window in range(SNAPS):
        phase_now = snap_phase[window]
        empty_snapshot = jnp.zeros_like(current)

        def one_step(local_index, carried):
            current, previous, snapshot = carried
            step_index = window * SNAP_EVERY + local_index
            extended = extended_2(current, (("gz", 1),), 4)
            faces_now = lax.dynamic_index_in_dim(
                saved_faces, face_steps[step_index], 0, keepdims=False
            )
            trace_now = lax.dynamic_index_in_dim(traces, step_index, 0, keepdims=False).astype(
                jnp.float32
            )
            updated = advance(
                extended, current, previous, speed_term, faces_now, trace_now, top_row, layers
            )
            snapshot = jnp.where(local_index == phase_now, updated, snapshot)
            return (updated, current, snapshot)

        current, previous, snapshot = lax.fori_loop(
            0, SNAP_EVERY, one_step, (current, previous, empty_snapshot)
        )
        columns_now = lax.all_to_all(snapshot, "gz", split_axis=2, concat_axis=1, tiled=True)
        raw_now, light_now = lag_images(columns_now, lag_offsets)
        if window == 0:
            raw_image = raw_now
            illumination = light_now
        else:
            raw_image = raw_image + raw_now
            illumination = illumination + light_now
    return (finish(raw_image, illumination), current[0], current[1])


def solution(mesh):
    return jax.shard_map(
        local,
        mesh=mesh,
        in_specs=(
            P(("shot", "gz"), None, None),
            P(("shot", "gz"), None, None),
            P(("shot", "gz"), None, None),
            P(("shot", "gz"), None, None),
            P("gz", None, None),
            P("shot", None, "gz", None),
            P(),
            P("shot", None, None),
            P(),
            P(),
        ),
        out_specs=(
            P("shot", None, "gz", None),
            P(("shot", "gz"), None, None),
            P(("shot", "gz"), None, None),
        ),
        check_vma=False,
    )
```

profile of v0, /device:TPU:9, one launch (start us, length us, event | category | flops | bytes accessed | tf_op | source)
XLA Modules:
  0.0 345.8 jit_solution(5449457502616833850)
XLA Ops:
  5.8 135.9 %while.44 = (s32[]{:T(128)}, f32[2,8,128,128]{3,2,1,0:T(8,128)S(1)}, f32[2,8,128,128]{3,2,1,0:T(8,128)S(1)}, f32[2,8,128,128]{3,2,1,0:T(8,128)}, s32[12]{0:T(128...) while((s32[]{:T(128)}, ...), condition=%wide.region_1.2_spmd.clone, body=%wide.region_0.1_spmd.clone.sunk | while | flops 24529312 | bytes 40568852 | solution.py:152
  6.8 3.7 %collective-permute-start = (f32[2,4,128,128]{3,2,1,0:T(8,128)}, f32[2,4,128,128]{3,2,1,0:T(8,128)}, u32[]{:S(2)}, u32[]{:S(2)}) collective-permute-start(f32[2,4,128,128]{3,2,1,0:T(8,128)} %get-tuple-element.965), channel_id=1, source_target_pairs={{0,1},{1,2},{2,3},{3,4},{4,5},{5,6},{6,7},{7,8},{8,9},{9,10},{10,1... | collective-permute-start | bytes 1572872 | tf_op jit(solution)/shard_map/while/body/eval_jaxpr/ppermute | solution.py:21
  10.5 1.9 collective-permute-start.1
  16.4 6.2 %collective-permute-done = f32[2,4,128,128]{3,2,1,0:T(8,128)} collective-permute-done((f32[2,4,128,128]{3,2,1,0:T(8,128)}, f32[2,4,128,128]{3,2,1,0:T(8,128)}, u32[]{:S(2)}, u32[]{:S(2)}) %collective-permute-start) | collective-permute-done | bytes 524320 | tf_op jit(solution)/shard_map/while/body/eval_jaxpr/ppermute | solution.py:21
  24.1 2.4 fusion.183
  30.2 4.3 %collective-permute-start = (f32[2,4,128,128]{3,2,1,0:T(8,128)}, f32[2,4,128,128]{3,2,1,0:T(8,128)}, u32[]{:S(2)}, u32[]{:S(2)}) collective-permute-start(f32[2,4,128,128]{3,2,1,0:T(8,128)} %get-tuple-element.965), channel_id=1, source_target_pairs={{0,1},{1,2},{2,3},{3,4},{4,5},{5,6},{6,7},{7,8},{8,9},{9,10},{10,1... | collective-permute-start | bytes 1572872 | tf_op jit(solution)/shard_map/while/body/eval_jaxpr/ppermute | solution.py:21
  34.4 1.9 collective-permute-start.1
  40.2 6.2 %collective-permute-done = f32[2,4,128,128]{3,2,1,0:T(8,128)} collective-permute-done((f32[2,4,128,128]{3,2,1,0:T(8,128)}, f32[2,4,128,128]{3,2,1,0:T(8,128)}, u32[]{:S(2)}, u32[]{:S(2)}) %collective-permute-start) | collective-permute-done | bytes 524320 | tf_op jit(solution)/shard_map/while/body/eval_jaxpr/ppermute | solution.py:21
  47.8 2.4 fusion.183
  53.9 4.4 %collective-permute-start = (f32[2,4,128,128]{3,2,1,0:T(8,128)}, f32[2,4,128,128]{3,2,1,0:T(8,128)}, u32[]{:S(2)}, u32[]{:S(2)}) collective-permute-start(f32[2,4,128,128]{3,2,1,0:T(8,128)} %get-tuple-element.965), channel_id=1, source_target_pairs={{0,1},{1,2},{2,3},{3,4},{4,5},{5,6},{6,7},{7,8},{8,9},{9,10},{10,1... | collective-permute-start | bytes 1572872 | tf_op jit(solution)/shard_map/while/body/eval_jaxpr/ppermute | solution.py:21
  58.3 1.9 collective-permute-start.1
  64.1 6.2 %collective-permute-done = f32[2,4,128,128]{3,2,1,0:T(8,128)} collective-permute-done((f32[2,4,128,128]{3,2,1,0:T(8,128)}, f32[2,4,128,128]{3,2,1,0:T(8,128)}, u32[]{:S(2)}, u32[]{:S(2)}) %collective-permute-start) | collective-permute-done | bytes 524320 | tf_op jit(solution)/shard_map/while/body/eval_jaxpr/ppermute | solution.py:21
  71.7 2.4 fusion.183
  77.8 4.4 %collective-permute-start = (f32[2,4,128,128]{3,2,1,0:T(8,128)}, f32[2,4,128,128]{3,2,1,0:T(8,128)}, u32[]{:S(2)}, u32[]{:S(2)}) collective-permute-start(f32[2,4,128,128]{3,2,1,0:T(8,128)} %get-tuple-element.965), channel_id=1, source_target_pairs={{0,1},{1,2},{2,3},{3,4},{4,5},{5,6},{6,7},{7,8},{8,9},{9,10},{10,1... | collective-permute-start | bytes 1572872 | tf_op jit(solution)/shard_map/while/body/eval_jaxpr/ppermute | solution.py:21
  82.2 1.9 collective-permute-start.1
  88.0 4.7 %collective-permute-done = f32[2,4,128,128]{3,2,1,0:T(8,128)} collective-permute-done((f32[2,4,128,128]{3,2,1,0:T(8,128)}, f32[2,4,128,128]{3,2,1,0:T(8,128)}, u32[]{:S(2)}, u32[]{:S(2)}) %collective-permute-start) | collective-permute-done | bytes 524320 | tf_op jit(solution)/shard_map/while/body/eval_jaxpr/ppermute | solution.py:21
  94.1 2.4 fusion.183
  100.1 4.4 %collective-permute-start = (f32[2,4,128,128]{3,2,1,0:T(8,128)}, f32[2,4,128,128]{3,2,1,0:T(8,128)}, u32[]{:S(2)}, u32[]{:S(2)}) collective-permute-start(f32[2,4,128,128]{3,2,1,0:T(8,128)} %get-tuple-element.965), channel_id=1, source_target_pairs={{0,1},{1,2},{2,3},{3,4},{4,5},{5,6},{6,7},{7,8},{8,9},{9,10},{10,1... | collective-permute-start | bytes 1572872 | tf_op jit(solution)/shard_map/while/body/eval_jaxpr/ppermute | solution.py:21
  104.5 1.9 collective-permute-start.1
  110.3 3.7 %collective-permute-done = f32[2,4,128,128]{3,2,1,0:T(8,128)} collective-permute-done((f32[2,4,128,128]{3,2,1,0:T(8,128)}, f32[2,4,128,128]{3,2,1,0:T(8,128)}, u32[]{:S(2)}, u32[]{:S(2)}) %collective-permute-start) | collective-permute-done | bytes 524320 | tf_op jit(solution)/shard_map/while/body/eval_jaxpr/ppermute | solution.py:21
  115.4 2.4 fusion.183
  121.5 4.4 %collective-permute-start = (f32[2,4,128,128]{3,2,1,0:T(8,128)}, f32[2,4,128,128]{3,2,1,0:T(8,128)}, u32[]{:S(2)}, u32[]{:S(2)}) collective-permute-start(f32[2,4,128,128]{3,2,1,0:T(8,128)} %get-tuple-element.965), channel_id=1, source_target_pairs={{0,1},{1,2},{2,3},{3,4},{4,5},{5,6},{6,7},{7,8},{8,9},{9,10},{10,1... | collective-permute-start | bytes 1572872 | tf_op jit(solution)/shard_map/while/body/eval_jaxpr/ppermute | solution.py:21
  125.9 1.9 collective-permute-start.1
  131.7 3.6 %collective-permute-done = f32[2,4,128,128]{3,2,1,0:T(8,128)} collective-permute-done((f32[2,4,128,128]{3,2,1,0:T(8,128)}, f32[2,4,128,128]{3,2,1,0:T(8,128)}, u32[]{:S(2)}, u32[]{:S(2)}) %collective-permute-start) | collective-permute-done | bytes 524320 | tf_op jit(solution)/shard_map/while/body/eval_jaxpr/ppermute | solution.py:21
  136.6 2.4 fusion.183
  141.6 128.2 %while.45 = (s32[]{:T(128)}, f32[2,8,128,128]{3,2,1,0:T(8,128)S(1)}, f32[2,8,128,128]{3,2,1,0:T(8,128)S(1)}, f32[2,8,128,128]{3,2,1,0:T(8,128)}, s32[12]{0:T(128...) while((s32[]{:T(128)}, ...), condition=%wide.region_3.4_spmd.clone, body=%wide.region_2.3_spmd.clone.sunk | while | flops 24529316 | bytes 40568908 | solution.py:152
  142.7 4.4 %collective-permute-start.2 = (f32[2,4,128,128]{3,2,1,0:T(8,128)}, f32[2,4,128,128]{3,2,1,0:T(8,128)}, u32[]{:S(2)}, u32[]{:S(2)}) collective-permute-start(f32[2,4,128,128]{3,2,1,0:T(8,128)} %get-tuple-element.981), channel_id=1, source_target_pairs={{0,1},{1,2},{2,3},{3,4},{4,5},{5,6},{6,7},{7,8},{8,9},{9,10},{10,1... | collective-permute-start | bytes 1572872 | tf_op jit(solution)/shard_map/while/body/eval_jaxpr/ppermute | solution.py:21
  153.0 3.6 %collective-permute-done.2 = f32[2,4,128,128]{3,2,1,0:T(8,128)} collective-permute-done((f32[2,4,128,128]{3,2,1,0:T(8,128)}, f32[2,4,128,128]{3,2,1,0:T(8,128)}, u32[]{:S(2)}, u32[]{:S(2)}) %collective-permute-start.2) | collective-permute-done | bytes 524320 | tf_op jit(solution)/shard_map/while/body/eval_jaxpr/ppermute | solution.py:21
  158.0 2.4 fusion.188
  164.1 4.4 %collective-permute-start.2 = (f32[2,4,128,128]{3,2,1,0:T(8,128)}, f32[2,4,128,128]{3,2,1,0:T(8,128)}, u32[]{:S(2)}, u32[]{:S(2)}) collective-permute-start(f32[2,4,128,128]{3,2,1,0:T(8,128)} %get-tuple-element.981), channel_id=1, source_target_pairs={{0,1},{1,2},{2,3},{3,4},{4,5},{5,6},{6,7},{7,8},{8,9},{9,10},{10,1... | collective-permute-start | bytes 1572872 | tf_op jit(solution)/shard_map/while/body/eval_jaxpr/ppermute | solution.py:21
  174.4 3.6 %collective-permute-done.2 = f32[2,4,128,128]{3,2,1,0:T(8,128)} collective-permute-done((f32[2,4,128,128]{3,2,1,0:T(8,128)}, f32[2,4,128,128]{3,2,1,0:T(8,128)}, u32[]{:S(2)}, u32[]{:S(2)}) %collective-permute-start.2) | collective-permute-done | bytes 524320 | tf_op jit(solution)/shard_map/while/body/eval_jaxpr/ppermute | solution.py:21
  179.3 2.4 fusion.188
  185.4 4.4 %collective-permute-start.2 = (f32[2,4,128,128]{3,2,1,0:T(8,128)}, f32[2,4,128,128]{3,2,1,0:T(8,128)}, u32[]{:S(2)}, u32[]{:S(2)}) collective-permute-start(f32[2,4,128,128]{3,2,1,0:T(8,128)} %get-tuple-element.981), channel_id=1, source_target_pairs={{0,1},{1,2},{2,3},{3,4},{4,5},{5,6},{6,7},{7,8},{8,9},{9,10},{10,1... | collective-permute-start | bytes 1572872 | tf_op jit(solution)/shard_map/while/body/eval_jaxpr/ppermute | solution.py:21
  195.7 3.6 %collective-permute-done.2 = f32[2,4,128,128]{3,2,1,0:T(8,128)} collective-permute-done((f32[2,4,128,128]{3,2,1,0:T(8,128)}, f32[2,4,128,128]{3,2,1,0:T(8,128)}, u32[]{:S(2)}, u32[]{:S(2)}) %collective-permute-start.2) | collective-permute-done | bytes 524320 | tf_op jit(solution)/shard_map/while/body/eval_jaxpr/ppermute | solution.py:21
  200.7 2.4 fusion.188
  206.8 4.4 %collective-permute-start.2 = (f32[2,4,128,128]{3,2,1,0:T(8,128)}, f32[2,4,128,128]{3,2,1,0:T(8,128)}, u32[]{:S(2)}, u32[]{:S(2)}) collective-permute-start(f32[2,4,128,128]{3,2,1,0:T(8,128)} %get-tuple-element.981), channel_id=1, source_target_pairs={{0,1},{1,2},{2,3},{3,4},{4,5},{5,6},{6,7},{7,8},{8,9},{9,10},{10,1... | collective-permute-start | bytes 1572872 | tf_op jit(solution)/shard_map/while/body/eval_jaxpr/ppermute | solution.py:21
  217.1 3.6 %collective-permute-done.2 = f32[2,4,128,128]{3,2,1,0:T(8,128)} collective-permute-done((f32[2,4,128,128]{3,2,1,0:T(8,128)}, f32[2,4,128,128]{3,2,1,0:T(8,128)}, u32[]{:S(2)}, u32[]{:S(2)}) %collective-permute-start.2) | collective-permute-done | bytes 524320 | tf_op jit(solution)/shard_map/while/body/eval_jaxpr/ppermute | solution.py:21
  222.0 2.4 fusion.188
  228.1 4.4 %collective-permute-start.2 = (f32[2,4,128,128]{3,2,1,0:T(8,128)}, f32[2,4,128,128]{3,2,1,0:T(8,128)}, u32[]{:S(2)}, u32[]{:S(2)}) collective-permute-start(f32[2,4,128,128]{3,2,1,0:T(8,128)} %get-tuple-element.981), channel_id=1, source_target_pairs={{0,1},{1,2},{2,3},{3,4},{4,5},{5,6},{6,7},{7,8},{8,9},{9,10},{10,1... | collective-permute-start | bytes 1572872 | tf_op jit(solution)/shard_map/while/body/eval_jaxpr/ppermute | solution.py:21
  238.4 3.6 %collective-permute-done.2 = f32[2,4,128,128]{3,2,1,0:T(8,128)} collective-permute-done((f32[2,4,128,128]{3,2,1,0:T(8,128)}, f32[2,4,128,128]{3,2,1,0:T(8,128)}, u32[]{:S(2)}, u32[]{:S(2)}) %collective-permute-start.2) | collective-permute-done | bytes 524320 | tf_op jit(solution)/shard_map/while/body/eval_jaxpr/ppermute | solution.py:21
  243.4 2.4 fusion.188
  249.5 4.4 %collective-permute-start.2 = (f32[2,4,128,128]{3,2,1,0:T(8,128)}, f32[2,4,128,128]{3,2,1,0:T(8,128)}, u32[]{:S(2)}, u32[]{:S(2)}) collective-permute-start(f32[2,4,128,128]{3,2,1,0:T(8,128)} %get-tuple-element.981), channel_id=1, source_target_pairs={{0,1},{1,2},{2,3},{3,4},{4,5},{5,6},{6,7},{7,8},{8,9},{9,10},{10,1... | collective-permute-start | bytes 1572872 | tf_op jit(solution)/shard_map/while/body/eval_jaxpr/ppermute | solution.py:21
  259.8 3.6 %collective-permute-done.2 = f32[2,4,128,128]{3,2,1,0:T(8,128)} collective-permute-done((f32[2,4,128,128]{3,2,1,0:T(8,128)}, f32[2,4,128,128]{3,2,1,0:T(8,128)}, u32[]{:S(2)}, u32[]{:S(2)}) %collective-permute-start.2) | collective-permute-done | bytes 524320 | tf_op jit(solution)/shard_map/while/body/eval_jaxpr/ppermute | solution.py:21
  264.8 2.4 fusion.188
  269.8 2.9 copy.32
  272.7 8.0 %all-to-all-start.1 = ((f32[2,8,128,128]{3,1,0,2:T(8,128)}), f32[2,8,128,128]{3,1,0,2:T(8,128)S(1)}, u32[]{:S(2)}, u32[]{:S(2)}) async-start(f32[2,8,128,128]{3,1,0,2:T(8,128)} %copy.32), calls=%async_computation.1 | async-start | bytes 2097152 | tf_op jit(solution)/shard_map/all_to_all | solution.py:155
  282.3 23.3 %all-to-all-done.1 = f32[2,8,128,128]{3,1,0,2:T(8,128)S(1)} async-done(((f32[2,8,128,128]{3,1,0,2:T(8,128)}), f32[2,8,128,128]{3,1,0,2:T(8,128)S(1)}, u32[]{:S(2)}, u32[]{:S(2)}) %all-to-all-start.1) | async-done | bytes 1048608 | tf_op jit(solution)/shard_map/all_to_all | solution.py:155
  305.6 4.8 %all-to-all-start = ((f32[2,8,128,128]{3,1,0,2:T(8,128)}), f32[2,8,128,128]{3,1,0,2:T(8,128)S(1)}, u32[]{:S(2)}, u32[]{:S(2)}) async-start(f32[2,8,128,128]{3,1,0,2:T(8,128)} %copy.29), calls=%async_computation | async-start | bytes 2097152 | tf_op jit(solution)/shard_map/all_to_all | solution.py:155
  (275 shorter events, 109.5 us)
Async XLA Ops:
  0.6 5.1 %copy-start.7 = (s32[12]{0:T(128)S(1)}, s32[12]{0:T(128)}, u32[]{:S(2)}) copy-start(s32[12]{0:T(128)} %param.20) | copy-start | bytes 148
  0.6 5.1 %copy-start = (f32[8,128,128]{2,1,0:T(8,128)S(1)}, f32[8,128,128]{2,1,0:T(8,128)}, u32[]{:S(2)}) copy-start(f32[8,128,128]{2,1,0:T(8,128)} %param.18) | copy-start | bytes 1572868
  6.8 15.7 %collective-permute-start = (f32[2,4,128,128]{3,2,1,0:T(8,128)}, f32[2,4,128,128]{3,2,1,0:T(8,128)}, u32[]{:S(2)}, u32[]{:S(2)}) collective-permute-start(f32[2,4,128,128]{3,2,1,0:T(8,128)} %get-tuple-element.965), channel_id=1, source_target_pairs={{0,1},{1,2},{2,3},{3,4},{4,5},{5,6},{6,7},{7,8},{8,9},{9,10},{10,1... | collective-permute-start | bytes 1572872 | tf_op jit(solution)/shard_map/while/body/eval_jaxpr/ppermute | solution.py:21
  10.5 13.5 %collective-permute-start.1 = (f32[2,4,128,128]{3,2,1,0:T(8,128)}, f32[2,4,128,128]{3,2,1,0:T(8,128)S(1)}, u32[]{:S(2)}, u32[]{:S(2)}) collective-permute-start(f32[2,4,128,128]{3,2,1,0:T(8,128)} %get-tuple-element.968), channel_id=1, source_target_pairs={{1,0},{2,1},{3,2},{4,3},{5,4},{6,5},{7,6},{8,7},{9,8},{10,9},{11,1... | collective-permute-start | bytes 1572872 | tf_op jit(solution)/shard_map/while/body/eval_jaxpr/ppermute | solution.py:24
  26.5 1.2 copy-start.3
  30.2 16.3 %collective-permute-start = (f32[2,4,128,128]{3,2,1,0:T(8,128)}, f32[2,4,128,128]{3,2,1,0:T(8,128)}, u32[]{:S(2)}, u32[]{:S(2)}) collective-permute-start(f32[2,4,128,128]{3,2,1,0:T(8,128)} %get-tuple-element.965), channel_id=1, source_target_pairs={{0,1},{1,2},{2,3},{3,4},{4,5},{5,6},{6,7},{7,8},{8,9},{9,10},{10,1... | collective-permute-start | bytes 1572872 | tf_op jit(solution)/shard_map/while/body/eval_jaxpr/ppermute | solution.py:21
  34.4 13.4 %collective-permute-start.1 = (f32[2,4,128,128]{3,2,1,0:T(8,128)}, f32[2,4,128,128]{3,2,1,0:T(8,128)S(1)}, u32[]{:S(2)}, u32[]{:S(2)}) collective-permute-start(f32[2,4,128,128]{3,2,1,0:T(8,128)} %get-tuple-element.968), channel_id=1, source_target_pairs={{1,0},{2,1},{3,2},{4,3},{5,4},{6,5},{7,6},{8,7},{9,8},{10,9},{11,1... | collective-permute-start | bytes 1572872 | tf_op jit(solution)/shard_map/while/body/eval_jaxpr/ppermute | solution.py:24
  50.2 1.2 copy-start.3
  53.9 16.4 %collective-permute-start = (f32[2,4,128,128]{3,2,1,0:T(8,128)}, f32[2,4,128,128]{3,2,1,0:T(8,128)}, u32[]{:S(2)}, u32[]{:S(2)}) collective-permute-start(f32[2,4,128,128]{3,2,1,0:T(8,128)} %get-tuple-element.965), channel_id=1, source_target_pairs={{0,1},{1,2},{2,3},{3,4},{4,5},{5,6},{6,7},{7,8},{8,9},{9,10},{10,1... | collective-permute-start | bytes 1572872 | tf_op jit(solution)/shard_map/while/body/eval_jaxpr/ppermute | solution.py:21
  58.3 13.4 %collective-permute-start.1 = (f32[2,4,128,128]{3,2,1,0:T(8,128)}, f32[2,4,128,128]{3,2,1,0:T(8,128)S(1)}, u32[]{:S(2)}, u32[]{:S(2)}) collective-permute-start(f32[2,4,128,128]{3,2,1,0:T(8,128)} %get-tuple-element.968), channel_id=1, source_target_pairs={{1,0},{2,1},{3,2},{4,3},{5,4},{6,5},{7,6},{8,7},{9,8},{10,9},{11,1... | collective-permute-start | bytes 1572872 | tf_op jit(solution)/shard_map/while/body/eval_jaxpr/ppermute | solution.py:24
  74.1 1.2 copy-start.3
  77.8 14.9 %collective-permute-start = (f32[2,4,128,128]{3,2,1,0:T(8,128)}, f32[2,4,128,128]{3,2,1,0:T(8,128)}, u32[]{:S(2)}, u32[]{:S(2)}) collective-permute-start(f32[2,4,128,128]{3,2,1,0:T(8,128)} %get-tuple-element.965), channel_id=1, source_target_pairs={{0,1},{1,2},{2,3},{3,4},{4,5},{5,6},{6,7},{7,8},{8,9},{9,10},{10,1... | collective-permute-start | bytes 1572872 | tf_op jit(solution)/shard_map/while/body/eval_jaxpr/ppermute | solution.py:21
  82.2 11.8 %collective-permute-start.1 = (f32[2,4,128,128]{3,2,1,0:T(8,128)}, f32[2,4,128,128]{3,2,1,0:T(8,128)S(1)}, u32[]{:S(2)}, u32[]{:S(2)}) collective-permute-start(f32[2,4,128,128]{3,2,1,0:T(8,128)} %get-tuple-element.968), channel_id=1, source_target_pairs={{1,0},{2,1},{3,2},{4,3},{5,4},{6,5},{7,6},{8,7},{9,8},{10,9},{11,1... | collective-permute-start | bytes 1572872 | tf_op jit(solution)/shard_map/while/body/eval_jaxpr/ppermute | solution.py:24
  96.5 1.2 copy-start.3
  100.1 13.9 %collective-permute-start = (f32[2,4,128,128]{3,2,1,0:T(8,128)}, f32[2,4,128,128]{3,2,1,0:T(8,128)}, u32[]{:S(2)}, u32[]{:S(2)}) collective-permute-start(f32[2,4,128,128]{3,2,1,0:T(8,128)} %get-tuple-element.965), channel_id=1, source_target_pairs={{0,1},{1,2},{2,3},{3,4},{4,5},{5,6},{6,7},{7,8},{8,9},{9,10},{10,1... | collective-permute-start | bytes 1572872 | tf_op jit(solution)/shard_map/while/body/eval_jaxpr/ppermute | solution.py:21
  104.5 10.8 %collective-permute-start.1 = (f32[2,4,128,128]{3,2,1,0:T(8,128)}, f32[2,4,128,128]{3,2,1,0:T(8,128)S(1)}, u32[]{:S(2)}, u32[]{:S(2)}) collective-permute-start(f32[2,4,128,128]{3,2,1,0:T(8,128)} %get-tuple-element.968), channel_id=1, source_target_pairs={{1,0},{2,1},{3,2},{4,3},{5,4},{6,5},{7,6},{8,7},{9,8},{10,9},{11,1... | collective-permute-start | bytes 1572872 | tf_op jit(solution)/shard_map/while/body/eval_jaxpr/ppermute | solution.py:24
  117.8 1.2 copy-start.3
  121.5 13.8 %collective-permute-start = (f32[2,4,128,128]{3,2,1,0:T(8,128)}, f32[2,4,128,128]{3,2,1,0:T(8,128)}, u32[]{:S(2)}, u32[]{:S(2)}) collective-permute-start(f32[2,4,128,128]{3,2,1,0:T(8,128)} %get-tuple-element.965), channel_id=1, source_target_pairs={{0,1},{1,2},{2,3},{3,4},{4,5},{5,6},{6,7},{7,8},{8,9},{9,10},{10,1... | collective-permute-start | bytes 1572872 | tf_op jit(solution)/shard_map/while/body/eval_jaxpr/ppermute | solution.py:21
  125.9 10.7 %collective-permute-start.1 = (f32[2,4,128,128]{3,2,1,0:T(8,128)}, f32[2,4,128,128]{3,2,1,0:T(8,128)S(1)}, u32[]{:S(2)}, u32[]{:S(2)}) collective-permute-start(f32[2,4,128,128]{3,2,1,0:T(8,128)} %get-tuple-element.968), channel_id=1, source_target_pairs={{1,0},{2,1},{3,2},{4,3},{5,4},{6,5},{7,6},{8,7},{9,8},{10,9},{11,1... | collective-permute-start | bytes 1572872 | tf_op jit(solution)/shard_map/while/body/eval_jaxpr/ppermute | solution.py:24
  139.1 1.2 copy-start.3
  142.7 13.9 %collective-permute-start.2 = (f32[2,4,128,128]{3,2,1,0:T(8,128)}, f32[2,4,128,128]{3,2,1,0:T(8,128)}, u32[]{:S(2)}, u32[]{:S(2)}) collective-permute-start(f32[2,4,128,128]{3,2,1,0:T(8,128)} %get-tuple-element.981), channel_id=1, source_target_pairs={{0,1},{1,2},{2,3},{3,4},{4,5},{5,6},{6,7},{7,8},{8,9},{9,10},{10,1... | collective-permute-start | bytes 1572872 | tf_op jit(solution)/shard_map/while/body/eval_jaxpr/ppermute | solution.py:21
  147.1 10.8 %collective-permute-start.3 = (f32[2,4,128,128]{3,2,1,0:T(8,128)}, f32[2,4,128,128]{3,2,1,0:T(8,128)S(1)}, u32[]{:S(2)}, u32[]{:S(2)}) collective-permute-start(f32[2,4,128,128]{3,2,1,0:T(8,128)} %get-tuple-element.984), channel_id=1, source_target_pairs={{1,0},{2,1},{3,2},{4,3},{5,4},{6,5},{7,6},{8,7},{9,8},{10,9},{11,1... | collective-permute-start | bytes 1572872 | tf_op jit(solution)/shard_map/while/body/eval_jaxpr/ppermute | solution.py:24
  160.4 1.2 copy-start.1
  162.0 1.0 copy-start.2
  164.1 13.8 %collective-permute-start.2 = (f32[2,4,128,128]{3,2,1,0:T(8,128)}, f32[2,4,128,128]{3,2,1,0:T(8,128)}, u32[]{:S(2)}, u32[]{:S(2)}) collective-permute-start(f32[2,4,128,128]{3,2,1,0:T(8,128)} %get-tuple-element.981), channel_id=1, source_target_pairs={{0,1},{1,2},{2,3},{3,4},{4,5},{5,6},{6,7},{7,8},{8,9},{9,10},{10,1... | collective-permute-start | bytes 1572872 | tf_op jit(solution)/shard_map/while/body/eval_jaxpr/ppermute | solution.py:21
  168.5 10.8 %collective-permute-start.3 = (f32[2,4,128,128]{3,2,1,0:T(8,128)}, f32[2,4,128,128]{3,2,1,0:T(8,128)S(1)}, u32[]{:S(2)}, u32[]{:S(2)}) collective-permute-start(f32[2,4,128,128]{3,2,1,0:T(8,128)} %get-tuple-element.984), channel_id=1, source_target_pairs={{1,0},{2,1},{3,2},{4,3},{5,4},{6,5},{7,6},{8,7},{9,8},{10,9},{11,1... | collective-permute-start | bytes 1572872 | tf_op jit(solution)/shard_map/while/body/eval_jaxpr/ppermute | solution.py:24
  181.7 1.2 copy-start.1
  183.3 1.0 copy-start.2
  185.4 13.9 %collective-permute-start.2 = (f32[2,4,128,128]{3,2,1,0:T(8,128)}, f32[2,4,128,128]{3,2,1,0:T(8,128)}, u32[]{:S(2)}, u32[]{:S(2)}) collective-permute-start(f32[2,4,128,128]{3,2,1,0:T(8,128)} %get-tuple-element.981), channel_id=1, source_target_pairs={{0,1},{1,2},{2,3},{3,4},{4,5},{5,6},{6,7},{7,8},{8,9},{9,10},{10,1... | collective-permute-start | bytes 1572872 | tf_op jit(solution)/shard_map/while/body/eval_jaxpr/ppermute | solution.py:21
  189.8 10.8 %collective-permute-start.3 = (f32[2,4,128,128]{3,2,1,0:T(8,128)}, f32[2,4,128,128]{3,2,1,0:T(8,128)S(1)}, u32[]{:S(2)}, u32[]{:S(2)}) collective-permute-start(f32[2,4,128,128]{3,2,1,0:T(8,128)} %get-tuple-element.984), channel_id=1, source_target_pairs={{1,0},{2,1},{3,2},{4,3},{5,4},{6,5},{7,6},{8,7},{9,8},{10,9},{11,1... | collective-permute-start | bytes 1572872 | tf_op jit(solution)/shard_map/while/body/eval_jaxpr/ppermute | solution.py:24
  203.1 1.2 copy-start.1
  204.7 1.0 copy-start.2
  206.8 13.8 %collective-permute-start.2 = (f32[2,4,128,128]{3,2,1,0:T(8,128)}, f32[2,4,128,128]{3,2,1,0:T(8,128)}, u32[]{:S(2)}, u32[]{:S(2)}) collective-permute-start(f32[2,4,128,128]{3,2,1,0:T(8,128)} %get-tuple-element.981), channel_id=1, source_target_pairs={{0,1},{1,2},{2,3},{3,4},{4,5},{5,6},{6,7},{7,8},{8,9},{9,10},{10,1... | collective-permute-start | bytes 1572872 | tf_op jit(solution)/shard_map/while/body/eval_jaxpr/ppermute | solution.py:21
  211.2 10.8 %collective-permute-start.3 = (f32[2,4,128,128]{3,2,1,0:T(8,128)}, f32[2,4,128,128]{3,2,1,0:T(8,128)S(1)}, u32[]{:S(2)}, u32[]{:S(2)}) collective-permute-start(f32[2,4,128,128]{3,2,1,0:T(8,128)} %get-tuple-element.984), channel_id=1, source_target_pairs={{1,0},{2,1},{3,2},{4,3},{5,4},{6,5},{7,6},{8,7},{9,8},{10,9},{11,1... | collective-permute-start | bytes 1572872 | tf_op jit(solution)/shard_map/while/body/eval_jaxpr/ppermute | solution.py:24
  224.5 1.2 copy-start.1
  226.1 1.0 copy-start.2
  228.1 13.9 %collective-permute-start.2 = (f32[2,4,128,128]{3,2,1,0:T(8,128)}, f32[2,4,128,128]{3,2,1,0:T(8,128)}, u32[]{:S(2)}, u32[]{:S(2)}) collective-permute-start(f32[2,4,128,128]{3,2,1,0:T(8,128)} %get-tuple-element.981), channel_id=1, source_target_pairs={{0,1},{1,2},{2,3},{3,4},{4,5},{5,6},{6,7},{7,8},{8,9},{9,10},{10,1... | collective-permute-start | bytes 1572872 | tf_op jit(solution)/shard_map/while/body/eval_jaxpr/ppermute | solution.py:21
  232.5 10.8 %collective-permute-start.3 = (f32[2,4,128,128]{3,2,1,0:T(8,128)}, f32[2,4,128,128]{3,2,1,0:T(8,128)S(1)}, u32[]{:S(2)}, u32[]{:S(2)}) collective-permute-start(f32[2,4,128,128]{3,2,1,0:T(8,128)} %get-tuple-element.984), channel_id=1, source_target_pairs={{1,0},{2,1},{3,2},{4,3},{5,4},{6,5},{7,6},{8,7},{9,8},{10,9},{11,1... | collective-permute-start | bytes 1572872 | tf_op jit(solution)/shard_map/while/body/eval_jaxpr/ppermute | solution.py:24
  245.9 1.2 copy-start.1
  247.5 1.0 copy-start.2
  249.5 13.8 %collective-permute-start.2 = (f32[2,4,128,128]{3,2,1,0:T(8,128)}, f32[2,4,128,128]{3,2,1,0:T(8,128)}, u32[]{:S(2)}, u32[]{:S(2)}) collective-permute-start(f32[2,4,128,128]{3,2,1,0:T(8,128)} %get-tuple-element.981), channel_id=1, source_target_pairs={{0,1},{1,2},{2,3},{3,4},{4,5},{5,6},{6,7},{7,8},{8,9},{9,10},{10,1... | collective-permute-start | bytes 1572872 | tf_op jit(solution)/shard_map/while/body/eval_jaxpr/ppermute | solution.py:21
  253.9 10.8 %collective-permute-start.3 = (f32[2,4,128,128]{3,2,1,0:T(8,128)}, f32[2,4,128,128]{3,2,1,0:T(8,128)S(1)}, u32[]{:S(2)}, u32[]{:S(2)}) collective-permute-start(f32[2,4,128,128]{3,2,1,0:T(8,128)} %get-tuple-element.984), channel_id=1, source_target_pairs={{1,0},{2,1},{3,2},{4,3},{5,4},{6,5},{7,6},{8,7},{9,8},{10,9},{11,1... | collective-permute-start | bytes 1572872 | tf_op jit(solution)/shard_map/while/body/eval_jaxpr/ppermute | solution.py:24
  267.2 1.2 copy-start.1
  268.8 1.0 copy-start.2
  269.8 10.9 %copy-start.5 = (f32[2,8,128,128]{3,2,1,0:T(8,128)S(1)}, f32[2,8,128,128]{3,2,1,0:T(8,128)}, u32[]{:S(2)}) copy-start(f32[2,8,128,128]{3,2,1,0:T(8,128)} %get-tuple-element.639) | copy-start | bytes 3145732
  269.8 40.6 %copy-start.6 = (s32[8]{0:T(128)S(1)}, s32[8]{0:T(128)}, u32[]{:S(2)}) copy-start(s32[8]{0:T(128)} %param.22) | copy-start | bytes 100
  272.7 33.0 %all-to-all-start.1 = ((f32[2,8,128,128]{3,1,0,2:T(8,128)}), f32[2,8,128,128]{3,1,0,2:T(8,128)S(1)}, u32[]{:S(2)}, u32[]{:S(2)}) async-start(f32[2,8,128,128]{3,1,0,2:T(8,128)} %copy.32), calls=%async_computation.1 | async-start | bytes 2097152 | tf_op jit(solution)/shard_map/all_to_all | solution.py:155
  305.6 29.7 %all-to-all-start = ((f32[2,8,128,128]{3,1,0,2:T(8,128)}), f32[2,8,128,128]{3,1,0,2:T(8,128)S(1)}, u32[]{:S(2)}, u32[]{:S(2)}) async-start(f32[2,8,128,128]{3,1,0,2:T(8,128)} %copy.29), calls=%async_computation | async-start | bytes 2097152 | tf_op jit(solution)/shard_map/all_to_all | solution.py:155
  (6 other events, 5.8 us)
where the time goes:
time: 349 us; the launch traced here: 346 us
  starting transfers between devices  87.6 us (25%)
  waiting for transfers between devices  77.2 us (22%)
  local copies, waits for them, and re-layouts  64.5 us (18%)
  other arithmetic  55.8 us (16%)
  loops' own time  31.6 us (9%)
  between operations  21.2 us (6%)
  matrix products  8.01 us (2%)
    ppermute x12, waiting for transfers between devices, extended_2(): lax.ppermute(lax.slice_in_dim(block, block.shape[dim] - width, None, axis...  52.2 us
    ppermute x12, starting transfers between devices, extended_2(): lax.ppermute(lax.slice_in_dim(block, block.shape[dim] - width, None, axis...  51.7 us
    while x84, local copies, waits for them, and re-layouts  33.2 us
    another operation x2, loops' own time, local(): lax.fori_loop(0, SNAP_EVERY, one_step, (current, previous, empty_snapshot))  31.6 us
    add x12, other arithmetic, advance(): updated = 2.0 * center - previous + speed_term * stencil(extended, layers)  29 us
    all_to_all x2, waiting for transfers between devices, local(): lax.all_to_all(snapshot, 'gz', split_axis=2, concat_axis=1, tiled=True)  24.8 us
    ppermute x12, starting transfers between devices, extended_2(): lax.ppermute(lax.slice_in_dim(block, 0, width, axis=dim), axis, backward)  23 us
    all_to_all x2, starting transfers between devices, local(): lax.all_to_all(snapshot, 'gz', split_axis=2, concat_axis=1, tiled=True)  12.8 us
  transfers between devices with their start and end apart: 26, of which 15 were waited for; matrix products, arithmetic and copies ran while one was open for 11% of the time, Pallas kernels for 0%

commit v1 on v0

--- a/solution.py
+++ b/solution.py
@@ -152,7 +152,10 @@
         current, previous, snapshot = lax.fori_loop(
             0, SNAP_EVERY, one_step, (current, previous, empty_snapshot)
         )
-        columns_now = lax.all_to_all(snapshot, "gz", split_axis=2, concat_axis=1, tiled=True)
+        columns_now = jnp.concatenate(
+            lax.all_to_all(jnp.stack(jnp.split(snapshot, lax.axis_size("gz"), axis=2)), "gz", 0, 0),
+            axis=1,
+        )
         raw_now, light_now = lag_images(columns_now, lag_offsets)
         if window == 0:
             raw_image = raw_now

time: 349 us -> 371 us (1.063)
  local copies, waits for them, and re-layouts: 64.5 us -> 92.7 us
  waiting for transfers between devices: 77.2 us -> 72.6 us
    unnamed x10 -> x42, local copies, waits for them, and re-layouts: 1.18 us -> 33.7 us
    all_to_all x2, waiting for transfers between devices: 24.8 us -> 18.1 us  [local(): lax.all_to_all(jnp.stack(jnp.split(snapshot, lax.axis_size('gz'), axis=2)...]
    while x86 -> x84, local copies, waits for them, and re-layouts: 37.7 us -> 33.1 us
  transfers between devices with their start and end apart: 26 -> 26, of which waited for: 15 -> 19; matrix products, arithmetic and copies ran while one was open for 11% -> 12% of each run, Pallas kernels for 0% -> 0%
where the time goes in v1:
time: 371 us; the launch traced here: 366 us
  local copies, waits for them, and re-layouts  92.7 us (25%)
  starting transfers between devices  87.2 us (24%)
  waiting for transfers between devices  72.6 us (20%)
  other arithmetic  55.8 us (15%)
  loops' own time  29.4 us (8%)
  between operations  20.7 us (6%)
  matrix products  8.01 us (2%)
    ppermute x12, waiting for transfers between devices, extended_2(): lax.ppermute(lax.slice_in_dim(block, block.shape[dim] - width, None, axis...  53.9 us
    ppermute x12, starting transfers between devices, extended_2(): lax.ppermute(lax.slice_in_dim(block, block.shape[dim] - width, None, axis...  51.3 us
    unnamed x42, local copies, waits for them, and re-layouts  33.7 us
    while x84, local copies, waits for them, and re-layouts  33.1 us
    another operation x2, loops' own time, local(): lax.fori_loop(0, SNAP_EVERY, one_step, (current, previous, empty_snapshot))  29.4 us
    add x12, other arithmetic, advance(): updated = 2.0 * center - previous + speed_term * stencil(extended, layers)  29 us
    ppermute x12, starting transfers between devices, extended_2(): lax.ppermute(lax.slice_in_dim(block, 0, width, axis=dim), axis, backward)  23 us
    all_to_all x2, waiting for transfers between devices, local(): lax.all_to_all(jnp.stack(jnp.split(snapshot, lax.axis_size('gz'), axis=2)...  18.1 us
  transfers between devices with their start and end apart: 26, of which 19 were waited for; matrix products, arithmetic and copies ran while one was open for 12% of the time, Pallas kernels for 0%

profile of v1, /device:TPU:9, one launch (start us, length us, event | category | flops | bytes accessed | tf_op | source)
XLA Modules:
  0.0 366.4 jit_solution(4616195983085457282)
XLA Ops:
  5.7 135.6 %while.44 = (s32[]{:T(128)}, f32[2,8,128,128]{3,2,1,0:T(8,128)S(1)}, f32[2,8,128,128]{3,2,1,0:T(8,128)S(1)}, f32[2,8,128,128]{3,2,1,0:T(8,128)}, s32[12]{0:T(128...) while((s32[]{:T(128)}, ...), condition=%wide.region_1.2_spmd.clone, body=%wide.region_0.1_spmd.clone.sunk | while | flops 24529312 | bytes 40568852 | solution.py:152
  6.7 3.7 %collective-permute-start = (f32[2,4,128,128]{3,2,1,0:T(8,128)}, f32[2,4,128,128]{3,2,1,0:T(8,128)}, u32[]{:S(2)}, u32[]{:S(2)}) collective-permute-start(f32[2,4,128,128]{3,2,1,0:T(8,128)} %get-tuple-element.925), channel_id=1, source_target_pairs={{0,1},{1,2},{2,3},{3,4},{4,5},{5,6},{6,7},{7,8},{8,9},{9,10},{10,1... | collective-permute-start | bytes 1572872 | tf_op jit(solution)/shard_map/while/body/eval_jaxpr/ppermute | solution.py:21
  10.5 1.9 collective-permute-start.1
  16.0 6.5 %collective-permute-done = f32[2,4,128,128]{3,2,1,0:T(8,128)} collective-permute-done((f32[2,4,128,128]{3,2,1,0:T(8,128)}, f32[2,4,128,128]{3,2,1,0:T(8,128)}, u32[]{:S(2)}, u32[]{:S(2)}) %collective-permute-start) | collective-permute-done | bytes 524320 | tf_op jit(solution)/shard_map/while/body/eval_jaxpr/ppermute | solution.py:21
  24.0 2.4 fusion.183
  30.1 4.3 %collective-permute-start = (f32[2,4,128,128]{3,2,1,0:T(8,128)}, f32[2,4,128,128]{3,2,1,0:T(8,128)}, u32[]{:S(2)}, u32[]{:S(2)}) collective-permute-start(f32[2,4,128,128]{3,2,1,0:T(8,128)} %get-tuple-element.925), channel_id=1, source_target_pairs={{0,1},{1,2},{2,3},{3,4},{4,5},{5,6},{6,7},{7,8},{8,9},{9,10},{10,1... | collective-permute-start | bytes 1572872 | tf_op jit(solution)/shard_map/while/body/eval_jaxpr/ppermute | solution.py:21
  34.3 1.9 collective-permute-start.1
  39.9 6.5 %collective-permute-done = f32[2,4,128,128]{3,2,1,0:T(8,128)} collective-permute-done((f32[2,4,128,128]{3,2,1,0:T(8,128)}, f32[2,4,128,128]{3,2,1,0:T(8,128)}, u32[]{:S(2)}, u32[]{:S(2)}) %collective-permute-start) | collective-permute-done | bytes 524320 | tf_op jit(solution)/shard_map/while/body/eval_jaxpr/ppermute | solution.py:21
  47.7 2.4 fusion.183
  53.8 4.4 %collective-permute-start = (f32[2,4,128,128]{3,2,1,0:T(8,128)}, f32[2,4,128,128]{3,2,1,0:T(8,128)}, u32[]{:S(2)}, u32[]{:S(2)}) collective-permute-start(f32[2,4,128,128]{3,2,1,0:T(8,128)} %get-tuple-element.925), channel_id=1, source_target_pairs={{0,1},{1,2},{2,3},{3,4},{4,5},{5,6},{6,7},{7,8},{8,9},{9,10},{10,1... | collective-permute-start | bytes 1572872 | tf_op jit(solution)/shard_map/while/body/eval_jaxpr/ppermute | solution.py:21
  58.2 1.9 collective-permute-start.1
  63.8 6.5 %collective-permute-done = f32[2,4,128,128]{3,2,1,0:T(8,128)} collective-permute-done((f32[2,4,128,128]{3,2,1,0:T(8,128)}, f32[2,4,128,128]{3,2,1,0:T(8,128)}, u32[]{:S(2)}, u32[]{:S(2)}) %collective-permute-start) | collective-permute-done | bytes 524320 | tf_op jit(solution)/shard_map/while/body/eval_jaxpr/ppermute | solution.py:21
  71.6 2.4 fusion.183
  77.7 4.4 %collective-permute-start = (f32[2,4,128,128]{3,2,1,0:T(8,128)}, f32[2,4,128,128]{3,2,1,0:T(8,128)}, u32[]{:S(2)}, u32[]{:S(2)}) collective-permute-start(f32[2,4,128,128]{3,2,1,0:T(8,128)} %get-tuple-element.925), channel_id=1, source_target_pairs={{0,1},{1,2},{2,3},{3,4},{4,5},{5,6},{6,7},{7,8},{8,9},{9,10},{10,1... | collective-permute-start | bytes 1572872 | tf_op jit(solution)/shard_map/while/body/eval_jaxpr/ppermute | solution.py:21
  82.1 1.9 collective-permute-start.1
  87.6 5.0 %collective-permute-done = f32[2,4,128,128]{3,2,1,0:T(8,128)} collective-permute-done((f32[2,4,128,128]{3,2,1,0:T(8,128)}, f32[2,4,128,128]{3,2,1,0:T(8,128)}, u32[]{:S(2)}, u32[]{:S(2)}) %collective-permute-start) | collective-permute-done | bytes 524320 | tf_op jit(solution)/shard_map/while/body/eval_jaxpr/ppermute | solution.py:21
  94.0 2.4 fusion.183
  100.0 4.4 %collective-permute-start = (f32[2,4,128,128]{3,2,1,0:T(8,128)}, f32[2,4,128,128]{3,2,1,0:T(8,128)}, u32[]{:S(2)}, u32[]{:S(2)}) collective-permute-start(f32[2,4,128,128]{3,2,1,0:T(8,128)} %get-tuple-element.925), channel_id=1, source_target_pairs={{0,1},{1,2},{2,3},{3,4},{4,5},{5,6},{6,7},{7,8},{8,9},{9,10},{10,1... | collective-permute-start | bytes 1572872 | tf_op jit(solution)/shard_map/while/body/eval_jaxpr/ppermute | solution.py:21
  104.4 1.9 collective-permute-start.1
  110.0 3.7 %collective-permute-done = f32[2,4,128,128]{3,2,1,0:T(8,128)} collective-permute-done((f32[2,4,128,128]{3,2,1,0:T(8,128)}, f32[2,4,128,128]{3,2,1,0:T(8,128)}, u32[]{:S(2)}, u32[]{:S(2)}) %collective-permute-start) | collective-permute-done | bytes 524320 | tf_op jit(solution)/shard_map/while/body/eval_jaxpr/ppermute | solution.py:21
  115.2 2.4 fusion.183
  121.3 4.3 %collective-permute-start = (f32[2,4,128,128]{3,2,1,0:T(8,128)}, f32[2,4,128,128]{3,2,1,0:T(8,128)}, u32[]{:S(2)}, u32[]{:S(2)}) collective-permute-start(f32[2,4,128,128]{3,2,1,0:T(8,128)} %get-tuple-element.925), channel_id=1, source_target_pairs={{0,1},{1,2},{2,3},{3,4},{4,5},{5,6},{6,7},{7,8},{8,9},{9,10},{10,1... | collective-permute-start | bytes 1572872 | tf_op jit(solution)/shard_map/while/body/eval_jaxpr/ppermute | solution.py:21
  125.5 1.9 collective-permute-start.1
  131.1 3.8 %collective-permute-done = f32[2,4,128,128]{3,2,1,0:T(8,128)} collective-permute-done((f32[2,4,128,128]{3,2,1,0:T(8,128)}, f32[2,4,128,128]{3,2,1,0:T(8,128)}, u32[]{:S(2)}, u32[]{:S(2)}) %collective-permute-start) | collective-permute-done | bytes 524320 | tf_op jit(solution)/shard_map/while/body/eval_jaxpr/ppermute | solution.py:21
  136.3 2.4 fusion.183
  141.3 127.6 %while.45 = (s32[]{:T(128)}, f32[2,8,128,128]{3,2,1,0:T(8,128)S(1)}, f32[2,8,128,128]{3,2,1,0:T(8,128)S(1)}, f32[2,8,128,128]{3,2,1,0:T(8,128)}, s32[12]{0:T(128...) while((s32[]{:T(128)}, ...), condition=%wide.region_3.4_spmd.clone, body=%wide.region_2.3_spmd.clone.sunk | while | flops 24529316 | bytes 40568908 | solution.py:152
  142.4 4.4 %collective-permute-start.2 = (f32[2,4,128,128]{3,2,1,0:T(8,128)}, f32[2,4,128,128]{3,2,1,0:T(8,128)}, u32[]{:S(2)}, u32[]{:S(2)}) collective-permute-start(f32[2,4,128,128]{3,2,1,0:T(8,128)} %get-tuple-element.941), channel_id=1, source_target_pairs={{0,1},{1,2},{2,3},{3,4},{4,5},{5,6},{6,7},{7,8},{8,9},{9,10},{10,1... | collective-permute-start | bytes 1572872 | tf_op jit(solution)/shard_map/while/body/eval_jaxpr/ppermute | solution.py:21
  152.5 3.5 collective-permute-done.2
  157.5 2.4 fusion.188
  163.6 4.3 %collective-permute-start.2 = (f32[2,4,128,128]{3,2,1,0:T(8,128)}, f32[2,4,128,128]{3,2,1,0:T(8,128)}, u32[]{:S(2)}, u32[]{:S(2)}) collective-permute-start(f32[2,4,128,128]{3,2,1,0:T(8,128)} %get-tuple-element.941), channel_id=1, source_target_pairs={{0,1},{1,2},{2,3},{3,4},{4,5},{5,6},{6,7},{7,8},{8,9},{9,10},{10,1... | collective-permute-start | bytes 1572872 | tf_op jit(solution)/shard_map/while/body/eval_jaxpr/ppermute | solution.py:21
  173.6 3.8 %collective-permute-done.2 = f32[2,4,128,128]{3,2,1,0:T(8,128)} collective-permute-done((f32[2,4,128,128]{3,2,1,0:T(8,128)}, f32[2,4,128,128]{3,2,1,0:T(8,128)}, u32[]{:S(2)}, u32[]{:S(2)}) %collective-permute-start.2) | collective-permute-done | bytes 524320 | tf_op jit(solution)/shard_map/while/body/eval_jaxpr/ppermute | solution.py:21
  178.8 2.4 fusion.188
  184.9 4.4 %collective-permute-start.2 = (f32[2,4,128,128]{3,2,1,0:T(8,128)}, f32[2,4,128,128]{3,2,1,0:T(8,128)}, u32[]{:S(2)}, u32[]{:S(2)}) collective-permute-start(f32[2,4,128,128]{3,2,1,0:T(8,128)} %get-tuple-element.941), channel_id=1, source_target_pairs={{0,1},{1,2},{2,3},{3,4},{4,5},{5,6},{6,7},{7,8},{8,9},{9,10},{10,1... | collective-permute-start | bytes 1572872 | tf_op jit(solution)/shard_map/while/body/eval_jaxpr/ppermute | solution.py:21
  195.1 3.5 collective-permute-done.2
  200.0 2.4 fusion.188
  206.1 4.3 %collective-permute-start.2 = (f32[2,4,128,128]{3,2,1,0:T(8,128)}, f32[2,4,128,128]{3,2,1,0:T(8,128)}, u32[]{:S(2)}, u32[]{:S(2)}) collective-permute-start(f32[2,4,128,128]{3,2,1,0:T(8,128)} %get-tuple-element.941), channel_id=1, source_target_pairs={{0,1},{1,2},{2,3},{3,4},{4,5},{5,6},{6,7},{7,8},{8,9},{9,10},{10,1... | collective-permute-start | bytes 1572872 | tf_op jit(solution)/shard_map/while/body/eval_jaxpr/ppermute | solution.py:21
  216.2 3.8 %collective-permute-done.2 = f32[2,4,128,128]{3,2,1,0:T(8,128)} collective-permute-done((f32[2,4,128,128]{3,2,1,0:T(8,128)}, f32[2,4,128,128]{3,2,1,0:T(8,128)}, u32[]{:S(2)}, u32[]{:S(2)}) %collective-permute-start.2) | collective-permute-done | bytes 524320 | tf_op jit(solution)/shard_map/while/body/eval_jaxpr/ppermute | solution.py:21
  221.4 2.4 fusion.188
  227.5 4.4 %collective-permute-start.2 = (f32[2,4,128,128]{3,2,1,0:T(8,128)}, f32[2,4,128,128]{3,2,1,0:T(8,128)}, u32[]{:S(2)}, u32[]{:S(2)}) collective-permute-start(f32[2,4,128,128]{3,2,1,0:T(8,128)} %get-tuple-element.941), channel_id=1, source_target_pairs={{0,1},{1,2},{2,3},{3,4},{4,5},{5,6},{6,7},{7,8},{8,9},{9,10},{10,1... | collective-permute-start | bytes 1572872 | tf_op jit(solution)/shard_map/while/body/eval_jaxpr/ppermute | solution.py:21
  237.6 3.5 collective-permute-done.2
  242.6 2.4 fusion.188
  248.7 4.3 %collective-permute-start.2 = (f32[2,4,128,128]{3,2,1,0:T(8,128)}, f32[2,4,128,128]{3,2,1,0:T(8,128)}, u32[]{:S(2)}, u32[]{:S(2)}) collective-permute-start(f32[2,4,128,128]{3,2,1,0:T(8,128)} %get-tuple-element.941), channel_id=1, source_target_pairs={{0,1},{1,2},{2,3},{3,4},{4,5},{5,6},{6,7},{7,8},{8,9},{9,10},{10,1... | collective-permute-start | bytes 1572872 | tf_op jit(solution)/shard_map/while/body/eval_jaxpr/ppermute | solution.py:21
  258.7 3.8 %collective-permute-done.2 = f32[2,4,128,128]{3,2,1,0:T(8,128)} collective-permute-done((f32[2,4,128,128]{3,2,1,0:T(8,128)}, f32[2,4,128,128]{3,2,1,0:T(8,128)}, u32[]{:S(2)}, u32[]{:S(2)}) %collective-permute-start.2) | collective-permute-done | bytes 524320 | tf_op jit(solution)/shard_map/while/body/eval_jaxpr/ppermute | solution.py:21
  263.9 2.4 fusion.188
  292.4 8.1 %all-to-all-start.1 = ((f32[16,2,8,8,128]{4,3,2,1,0:T(8,128)}), f32[16,2,8,8,128]{4,3,2,1,0:T(8,128)S(1)}, u32[]{:S(2)}, u32[]{:S(2)}) async-start(f32[16,2,8,8,128]{4,3,2,1,0:T(8,128)} %constant_dynamic-update-slice_fusion.24), calls=%async_computation.1 | async-start | bytes 2097152 | tf_op jit(solution)/shard_map/all_to_all | solution.py:156
  310.8 14.7 %all-to-all-done.1 = f32[16,2,8,8,128]{4,3,2,1,0:T(8,128)S(1)} async-done(((f32[16,2,8,8,128]{4,3,2,1,0:T(8,128)}), f32[16,2,8,8,128]{4,3,2,1,0:T(8,128)S(1)}, u32[]{:S(2)}, u32[]{:S(2)}) %all-to-all-start.1) | async-done | bytes 1048608 | tf_op jit(solution)/shard_map/all_to_all | solution.py:156
  325.5 4.8 %all-to-all-start = ((f32[16,2,8,8,128]{4,3,2,1,0:T(8,128)}), f32[16,2,8,8,128]{4,3,2,1,0:T(8,128)S(1)}, u32[]{:S(2)}, u32[]{:S(2)}) async-start(f32[16,2,8,8,128]{4,3,2,1,0:T(8,128)} %constant_dynamic-update-slice_fusion.8), calls=%async_computation | async-start | bytes 2097152 | tf_op jit(solution)/shard_map/all_to_all | solution.py:156
  351.8 3.4 all-to-all-done
  (305 shorter events, 139.7 us)
Async XLA Ops:
  0.6 5.0 %copy-start.8 = (s32[12]{0:T(128)S(1)}, s32[12]{0:T(128)}, u32[]{:S(2)}) copy-start(s32[12]{0:T(128)} %param.20) | copy-start | bytes 148
  0.6 5.0 %copy-start = (f32[8,128,128]{2,1,0:T(8,128)S(1)}, f32[8,128,128]{2,1,0:T(8,128)}, u32[]{:S(2)}) copy-start(f32[8,128,128]{2,1,0:T(8,128)} %param.18) | copy-start | bytes 1572868
  6.7 15.7 %collective-permute-start = (f32[2,4,128,128]{3,2,1,0:T(8,128)}, f32[2,4,128,128]{3,2,1,0:T(8,128)}, u32[]{:S(2)}, u32[]{:S(2)}) collective-permute-start(f32[2,4,128,128]{3,2,1,0:T(8,128)} %get-tuple-element.925), channel_id=1, source_target_pairs={{0,1},{1,2},{2,3},{3,4},{4,5},{5,6},{6,7},{7,8},{8,9},{9,10},{10,1... | collective-permute-start | bytes 1572872 | tf_op jit(solution)/shard_map/while/body/eval_jaxpr/ppermute | solution.py:21
  10.5 13.5 %collective-permute-start.1 = (f32[2,4,128,128]{3,2,1,0:T(8,128)}, f32[2,4,128,128]{3,2,1,0:T(8,128)S(1)}, u32[]{:S(2)}, u32[]{:S(2)}) collective-permute-start(f32[2,4,128,128]{3,2,1,0:T(8,128)} %get-tuple-element.928), channel_id=1, source_target_pairs={{1,0},{2,1},{3,2},{4,3},{5,4},{6,5},{7,6},{8,7},{9,8},{10,9},{11,1... | collective-permute-start | bytes 1572872 | tf_op jit(solution)/shard_map/while/body/eval_jaxpr/ppermute | solution.py:24
  26.4 1.2 copy-start.3
  30.1 16.3 %collective-permute-start = (f32[2,4,128,128]{3,2,1,0:T(8,128)}, f32[2,4,128,128]{3,2,1,0:T(8,128)}, u32[]{:S(2)}, u32[]{:S(2)}) collective-permute-start(f32[2,4,128,128]{3,2,1,0:T(8,128)} %get-tuple-element.925), channel_id=1, source_target_pairs={{0,1},{1,2},{2,3},{3,4},{4,5},{5,6},{6,7},{7,8},{8,9},{9,10},{10,1... | collective-permute-start | bytes 1572872 | tf_op jit(solution)/shard_map/while/body/eval_jaxpr/ppermute | solution.py:21
  34.3 13.4 %collective-permute-start.1 = (f32[2,4,128,128]{3,2,1,0:T(8,128)}, f32[2,4,128,128]{3,2,1,0:T(8,128)S(1)}, u32[]{:S(2)}, u32[]{:S(2)}) collective-permute-start(f32[2,4,128,128]{3,2,1,0:T(8,128)} %get-tuple-element.928), channel_id=1, source_target_pairs={{1,0},{2,1},{3,2},{4,3},{5,4},{6,5},{7,6},{8,7},{9,8},{10,9},{11,1... | collective-permute-start | bytes 1572872 | tf_op jit(solution)/shard_map/while/body/eval_jaxpr/ppermute | solution.py:24
  50.2 1.2 copy-start.3
  53.8 16.4 %collective-permute-start = (f32[2,4,128,128]{3,2,1,0:T(8,128)}, f32[2,4,128,128]{3,2,1,0:T(8,128)}, u32[]{:S(2)}, u32[]{:S(2)}) collective-permute-start(f32[2,4,128,128]{3,2,1,0:T(8,128)} %get-tuple-element.925), channel_id=1, source_target_pairs={{0,1},{1,2},{2,3},{3,4},{4,5},{5,6},{6,7},{7,8},{8,9},{9,10},{10,1... | collective-permute-start | bytes 1572872 | tf_op jit(solution)/shard_map/while/body/eval_jaxpr/ppermute | solution.py:21
  58.2 13.4 %collective-permute-start.1 = (f32[2,4,128,128]{3,2,1,0:T(8,128)}, f32[2,4,128,128]{3,2,1,0:T(8,128)S(1)}, u32[]{:S(2)}, u32[]{:S(2)}) collective-permute-start(f32[2,4,128,128]{3,2,1,0:T(8,128)} %get-tuple-element.928), channel_id=1, source_target_pairs={{1,0},{2,1},{3,2},{4,3},{5,4},{6,5},{7,6},{8,7},{9,8},{10,9},{11,1... | collective-permute-start | bytes 1572872 | tf_op jit(solution)/shard_map/while/body/eval_jaxpr/ppermute | solution.py:24
  74.0 1.2 copy-start.3
  77.7 14.9 %collective-permute-start = (f32[2,4,128,128]{3,2,1,0:T(8,128)}, f32[2,4,128,128]{3,2,1,0:T(8,128)}, u32[]{:S(2)}, u32[]{:S(2)}) collective-permute-start(f32[2,4,128,128]{3,2,1,0:T(8,128)} %get-tuple-element.925), channel_id=1, source_target_pairs={{0,1},{1,2},{2,3},{3,4},{4,5},{5,6},{6,7},{7,8},{8,9},{9,10},{10,1... | collective-permute-start | bytes 1572872 | tf_op jit(solution)/shard_map/while/body/eval_jaxpr/ppermute | solution.py:21
  82.1 11.8 %collective-permute-start.1 = (f32[2,4,128,128]{3,2,1,0:T(8,128)}, f32[2,4,128,128]{3,2,1,0:T(8,128)S(1)}, u32[]{:S(2)}, u32[]{:S(2)}) collective-permute-start(f32[2,4,128,128]{3,2,1,0:T(8,128)} %get-tuple-element.928), channel_id=1, source_target_pairs={{1,0},{2,1},{3,2},{4,3},{5,4},{6,5},{7,6},{8,7},{9,8},{10,9},{11,1... | collective-permute-start | bytes 1572872 | tf_op jit(solution)/shard_map/while/body/eval_jaxpr/ppermute | solution.py:24
  96.4 1.2 copy-start.3
  100.0 13.6 %collective-permute-start = (f32[2,4,128,128]{3,2,1,0:T(8,128)}, f32[2,4,128,128]{3,2,1,0:T(8,128)}, u32[]{:S(2)}, u32[]{:S(2)}) collective-permute-start(f32[2,4,128,128]{3,2,1,0:T(8,128)} %get-tuple-element.925), channel_id=1, source_target_pairs={{0,1},{1,2},{2,3},{3,4},{4,5},{5,6},{6,7},{7,8},{8,9},{9,10},{10,1... | collective-permute-start | bytes 1572872 | tf_op jit(solution)/shard_map/while/body/eval_jaxpr/ppermute | solution.py:21
  104.4 10.7 %collective-permute-start.1 = (f32[2,4,128,128]{3,2,1,0:T(8,128)}, f32[2,4,128,128]{3,2,1,0:T(8,128)S(1)}, u32[]{:S(2)}, u32[]{:S(2)}) collective-permute-start(f32[2,4,128,128]{3,2,1,0:T(8,128)} %get-tuple-element.928), channel_id=1, source_target_pairs={{1,0},{2,1},{3,2},{4,3},{5,4},{6,5},{7,6},{8,7},{9,8},{10,9},{11,1... | collective-permute-start | bytes 1572872 | tf_op jit(solution)/shard_map/while/body/eval_jaxpr/ppermute | solution.py:24
  117.6 1.2 copy-start.3
  121.3 13.6 %collective-permute-start = (f32[2,4,128,128]{3,2,1,0:T(8,128)}, f32[2,4,128,128]{3,2,1,0:T(8,128)}, u32[]{:S(2)}, u32[]{:S(2)}) collective-permute-start(f32[2,4,128,128]{3,2,1,0:T(8,128)} %get-tuple-element.925), channel_id=1, source_target_pairs={{0,1},{1,2},{2,3},{3,4},{4,5},{5,6},{6,7},{7,8},{8,9},{9,10},{10,1... | collective-permute-start | bytes 1572872 | tf_op jit(solution)/shard_map/while/body/eval_jaxpr/ppermute | solution.py:21
  125.5 10.7 %collective-permute-start.1 = (f32[2,4,128,128]{3,2,1,0:T(8,128)}, f32[2,4,128,128]{3,2,1,0:T(8,128)S(1)}, u32[]{:S(2)}, u32[]{:S(2)}) collective-permute-start(f32[2,4,128,128]{3,2,1,0:T(8,128)} %get-tuple-element.928), channel_id=1, source_target_pairs={{1,0},{2,1},{3,2},{4,3},{5,4},{6,5},{7,6},{8,7},{9,8},{10,9},{11,1... | collective-permute-start | bytes 1572872 | tf_op jit(solution)/shard_map/while/body/eval_jaxpr/ppermute | solution.py:24
  138.7 1.2 copy-start.3
  142.4 13.6 %collective-permute-start.2 = (f32[2,4,128,128]{3,2,1,0:T(8,128)}, f32[2,4,128,128]{3,2,1,0:T(8,128)}, u32[]{:S(2)}, u32[]{:S(2)}) collective-permute-start(f32[2,4,128,128]{3,2,1,0:T(8,128)} %get-tuple-element.941), channel_id=1, source_target_pairs={{0,1},{1,2},{2,3},{3,4},{4,5},{5,6},{6,7},{7,8},{8,9},{9,10},{10,1... | collective-permute-start | bytes 1572872 | tf_op jit(solution)/shard_map/while/body/eval_jaxpr/ppermute | solution.py:21
  146.7 10.7 %collective-permute-start.3 = (f32[2,4,128,128]{3,2,1,0:T(8,128)}, f32[2,4,128,128]{3,2,1,0:T(8,128)S(1)}, u32[]{:S(2)}, u32[]{:S(2)}) collective-permute-start(f32[2,4,128,128]{3,2,1,0:T(8,128)} %get-tuple-element.944), channel_id=1, source_target_pairs={{1,0},{2,1},{3,2},{4,3},{5,4},{6,5},{7,6},{8,7},{9,8},{10,9},{11,1... | collective-permute-start | bytes 1572872 | tf_op jit(solution)/shard_map/while/body/eval_jaxpr/ppermute | solution.py:24
  159.9 1.2 copy-start.1
  161.5 1.0 copy-start.2
  163.6 13.9 %collective-permute-start.2 = (f32[2,4,128,128]{3,2,1,0:T(8,128)}, f32[2,4,128,128]{3,2,1,0:T(8,128)}, u32[]{:S(2)}, u32[]{:S(2)}) collective-permute-start(f32[2,4,128,128]{3,2,1,0:T(8,128)} %get-tuple-element.941), channel_id=1, source_target_pairs={{0,1},{1,2},{2,3},{3,4},{4,5},{5,6},{6,7},{7,8},{8,9},{9,10},{10,1... | collective-permute-start | bytes 1572872 | tf_op jit(solution)/shard_map/while/body/eval_jaxpr/ppermute | solution.py:21
  167.9 10.9 %collective-permute-start.3 = (f32[2,4,128,128]{3,2,1,0:T(8,128)}, f32[2,4,128,128]{3,2,1,0:T(8,128)S(1)}, u32[]{:S(2)}, u32[]{:S(2)}) collective-permute-start(f32[2,4,128,128]{3,2,1,0:T(8,128)} %get-tuple-element.944), channel_id=1, source_target_pairs={{1,0},{2,1},{3,2},{4,3},{5,4},{6,5},{7,6},{8,7},{9,8},{10,9},{11,1... | collective-permute-start | bytes 1572872 | tf_op jit(solution)/shard_map/while/body/eval_jaxpr/ppermute | solution.py:24
  181.2 1.2 copy-start.1
  182.9 1.0 copy-start.2
  184.9 13.6 %collective-permute-start.2 = (f32[2,4,128,128]{3,2,1,0:T(8,128)}, f32[2,4,128,128]{3,2,1,0:T(8,128)}, u32[]{:S(2)}, u32[]{:S(2)}) collective-permute-start(f32[2,4,128,128]{3,2,1,0:T(8,128)} %get-tuple-element.941), channel_id=1, source_target_pairs={{0,1},{1,2},{2,3},{3,4},{4,5},{5,6},{6,7},{7,8},{8,9},{9,10},{10,1... | collective-permute-start | bytes 1572872 | tf_op jit(solution)/shard_map/while/body/eval_jaxpr/ppermute | solution.py:21
  189.3 10.7 %collective-permute-start.3 = (f32[2,4,128,128]{3,2,1,0:T(8,128)}, f32[2,4,128,128]{3,2,1,0:T(8,128)S(1)}, u32[]{:S(2)}, u32[]{:S(2)}) collective-permute-start(f32[2,4,128,128]{3,2,1,0:T(8,128)} %get-tuple-element.944), channel_id=1, source_target_pairs={{1,0},{2,1},{3,2},{4,3},{5,4},{6,5},{7,6},{8,7},{9,8},{10,9},{11,1... | collective-permute-start | bytes 1572872 | tf_op jit(solution)/shard_map/while/body/eval_jaxpr/ppermute | solution.py:24
  202.5 1.2 copy-start.1
  204.1 1.0 copy-start.2
  206.1 13.9 %collective-permute-start.2 = (f32[2,4,128,128]{3,2,1,0:T(8,128)}, f32[2,4,128,128]{3,2,1,0:T(8,128)}, u32[]{:S(2)}, u32[]{:S(2)}) collective-permute-start(f32[2,4,128,128]{3,2,1,0:T(8,128)} %get-tuple-element.941), channel_id=1, source_target_pairs={{0,1},{1,2},{2,3},{3,4},{4,5},{5,6},{6,7},{7,8},{8,9},{9,10},{10,1... | collective-permute-start | bytes 1572872 | tf_op jit(solution)/shard_map/while/body/eval_jaxpr/ppermute | solution.py:21
  210.4 10.9 %collective-permute-start.3 = (f32[2,4,128,128]{3,2,1,0:T(8,128)}, f32[2,4,128,128]{3,2,1,0:T(8,128)S(1)}, u32[]{:S(2)}, u32[]{:S(2)}) collective-permute-start(f32[2,4,128,128]{3,2,1,0:T(8,128)} %get-tuple-element.944), channel_id=1, source_target_pairs={{1,0},{2,1},{3,2},{4,3},{5,4},{6,5},{7,6},{8,7},{9,8},{10,9},{11,1... | collective-permute-start | bytes 1572872 | tf_op jit(solution)/shard_map/while/body/eval_jaxpr/ppermute | solution.py:24
  223.8 1.2 copy-start.1
  225.4 1.0 copy-start.2
  227.5 13.6 %collective-permute-start.2 = (f32[2,4,128,128]{3,2,1,0:T(8,128)}, f32[2,4,128,128]{3,2,1,0:T(8,128)}, u32[]{:S(2)}, u32[]{:S(2)}) collective-permute-start(f32[2,4,128,128]{3,2,1,0:T(8,128)} %get-tuple-element.941), channel_id=1, source_target_pairs={{0,1},{1,2},{2,3},{3,4},{4,5},{5,6},{6,7},{7,8},{8,9},{9,10},{10,1... | collective-permute-start | bytes 1572872 | tf_op jit(solution)/shard_map/while/body/eval_jaxpr/ppermute | solution.py:21
  231.8 10.7 %collective-permute-start.3 = (f32[2,4,128,128]{3,2,1,0:T(8,128)}, f32[2,4,128,128]{3,2,1,0:T(8,128)S(1)}, u32[]{:S(2)}, u32[]{:S(2)}) collective-permute-start(f32[2,4,128,128]{3,2,1,0:T(8,128)} %get-tuple-element.944), channel_id=1, source_target_pairs={{1,0},{2,1},{3,2},{4,3},{5,4},{6,5},{7,6},{8,7},{9,8},{10,9},{11,1... | collective-permute-start | bytes 1572872 | tf_op jit(solution)/shard_map/while/body/eval_jaxpr/ppermute | solution.py:24
  245.0 1.2 copy-start.1
  246.6 1.0 copy-start.2
  248.7 13.9 %collective-permute-start.2 = (f32[2,4,128,128]{3,2,1,0:T(8,128)}, f32[2,4,128,128]{3,2,1,0:T(8,128)}, u32[]{:S(2)}, u32[]{:S(2)}) collective-permute-start(f32[2,4,128,128]{3,2,1,0:T(8,128)} %get-tuple-element.941), channel_id=1, source_target_pairs={{0,1},{1,2},{2,3},{3,4},{4,5},{5,6},{6,7},{7,8},{8,9},{9,10},{10,1... | collective-permute-start | bytes 1572872 | tf_op jit(solution)/shard_map/while/body/eval_jaxpr/ppermute | solution.py:21
  253.0 10.9 %collective-permute-start.3 = (f32[2,4,128,128]{3,2,1,0:T(8,128)}, f32[2,4,128,128]{3,2,1,0:T(8,128)S(1)}, u32[]{:S(2)}, u32[]{:S(2)}) collective-permute-start(f32[2,4,128,128]{3,2,1,0:T(8,128)} %get-tuple-element.944), channel_id=1, source_target_pairs={{1,0},{2,1},{3,2},{4,3},{5,4},{6,5},{7,6},{8,7},{9,8},{10,9},{11,1... | collective-permute-start | bytes 1572872 | tf_op jit(solution)/shard_map/while/body/eval_jaxpr/ppermute | solution.py:24
  266.3 1.2 copy-start.1
  267.9 1.0 copy-start.2
  268.9 31.7 %copy-start.5 = (f32[2,8,128,128]{3,2,1,0:T(8,128)S(1)}, f32[2,8,128,128]{3,2,1,0:T(8,128)}, u32[]{:S(2)}) copy-start(f32[2,8,128,128]{3,2,1,0:T(8,128)} %get-tuple-element.639) | copy-start | bytes 3145732
  268.9 61.3 %copy-start.7 = (s32[8]{0:T(128)S(1)}, s32[8]{0:T(128)}, u32[]{:S(2)}) copy-start(s32[8]{0:T(128)} %param.22) | copy-start | bytes 100
  292.4 33.1 %all-to-all-start.1 = ((f32[16,2,8,8,128]{4,3,2,1,0:T(8,128)}), f32[16,2,8,8,128]{4,3,2,1,0:T(8,128)S(1)}, u32[]{:S(2)}, u32[]{:S(2)}) async-start(f32[16,2,8,8,128]{4,3,2,1,0:T(8,128)} %constant_dynamic-update-slice_fusion.24), calls=%async_computation.1 | async-start | bytes 2097152 | tf_op jit(solution)/shard_map/all_to_all | solution.py:156
  325.5 29.7 %all-to-all-start = ((f32[16,2,8,8,128]{4,3,2,1,0:T(8,128)}), f32[16,2,8,8,128]{4,3,2,1,0:T(8,128)S(1)}, u32[]{:S(2)}, u32[]{:S(2)}) async-start(f32[16,2,8,8,128]{4,3,2,1,0:T(8,128)} %constant_dynamic-update-slice_fusion.8), calls=%async_computation | async-start | bytes 2097152 | tf_op jit(solution)/shard_map/all_to_all | solution.py:156
  (7 other events, 6.8 us)
